TPU v7x, 128 devices: a whole 4x4x4 slice. The times are simulated.
128 devices in a mesh: dp: 16 (over x_lo, z, core), loop: 8 (over x_hi, y).
Axes of the slice: x: 4 (x_hi: 2, x_lo: 2; x = x_hi * 2 + x_lo), y: 4, z: 4, core: 2. Of those that a mesh axis runs over, the one named last changes fastest.
Arguments:
- crop_tokens: bfloat16 [8192, 64, 1152], P(('dp', 'loop')), may hold values from -6 to 6
- crop_lengths: int32 [128, 64], P(('dp', 'loop')), may hold values from 1 to 64, 3072 in all within a row
- crop_owner: int32 [8192, 1], P(('dp', 'loop')), may hold values from 0 to 15; in each aligned block of 64 rows (0 to 63, 64 to 127, ...) at most 8 rows name the same one
- crop_slot: int32 [8192], P(('dp', 'loop')), may hold values from 0 to 31
- base_tokens: bfloat16 [4096, 32, 1152], P(('dp', 'loop')), may hold values from -1024 to 1024
- key_probe: bfloat16 [1152, 16], replicated, may hold values from -1 to 1
- value_weight: bfloat16 [1152, 1152], replicated, may hold values from -0.1875 to 0.1875
- out_weight: bfloat16 [1152, 1152], replicated, may hold values from -0.1875 to 0.1875
- text_embed: bfloat16 [4096, 1152], P(('dp', 'loop')), may hold values from -6 to 6
- pair_labels: int32 [4096], P(('dp', 'loop')), may hold values from 0 to 63
- logit_scale: float32 [1], replicated, may hold values from 2 to 8
- logit_bias: float32 [1], replicated, may hold values from -4 to -1
Outputs:
- image_embed: bfloat16 [4096, 1152], P(('dp', 'loop'))
- image_grad: float32 [4096, 1152], P(('dp', 'loop'))
- text_grad: float32 [4096, 1152], P(('dp', 'loop'))
Inputs may be any that keep to these rules, and one draw needn't show every extreme that they name: `crop_owner`: at most 8 of the crops of one device name the same owner, and in every draw the crops of some device name one owner exactly 8 times. `crop_lengths`: the lengths of one device's crops sum to 3072 and the longest is exactly 64.
All inputs are finite; a program needn't handle non-finite values.
Results may differ from a plain program's by a relative error of at most 0.01.
Values may be sent and summed in bfloat16 or wider, within the bound.
No kernel may reach another device: no remote copies, remote signals or barrier semaphores. Data moves between devices by JAX's collectives and lax.ppermute only.
A program may use at most 192 MiB of HBM per device.

v0:
```python
import math

import jax
import jax.numpy as jnp
from jax import lax
from jax.sharding import PartitionSpec as P

very_low = -1e30
norm_eps = 1e-06
highest = lax.Precision.HIGHEST


def crop_partial(tokens, lengths, key_probe, value_weight):
    lead_shape = tokens.shape[:-2]
    crop_width = tokens.shape[-2]
    model_width = tokens.shape[-1]
    head_count = key_probe.shape[1]
    head_dim = model_width // head_count
    flat_rows = tokens.reshape(-1, model_width)
    scores = jnp.dot(flat_rows, key_probe, preferred_element_type=jnp.float32) / math.sqrt(head_dim)
    scores = scores.reshape(lead_shape + (crop_width, head_count))
    position = lax.broadcasted_iota(jnp.int32, lead_shape + (crop_width,), len(lead_shape))
    is_valid = (position < lengths[..., None])[..., None]
    masked = jnp.where(is_valid, scores, very_low)
    maxima = jnp.max(masked, axis=-2)
    weight = jnp.where(is_valid, jnp.exp(masked - maxima[..., None, :]), 0.0)
    totals = jnp.sum(weight, axis=-2)
    mixed = jnp.einsum("...kh,...kd->...hd", weight, tokens.astype(jnp.float32), precision=highest)
    value_heads = value_weight.astype(jnp.float32).reshape(model_width, head_count, head_dim)
    projected = jnp.einsum("...hd,dhe->...he", mixed, value_heads, precision=highest)
    return (projected.reshape(lead_shape + (model_width,)), maxima, totals)


def merge_parts(base_parts, arrived_parts, img_count):
    base_sum, base_max, base_total = base_parts
    mixed_sum, maxima, totals, slot_ids = arrived_parts
    slot_count, model_width = mixed_sum.shape
    head_count = maxima.shape[1]
    member = slot_ids[:, None] == lax.broadcasted_iota(jnp.int32, (1, img_count), 1)
    candidates = jnp.where(member[:, :, None], maxima[:, None, :], very_low)
    joint_max = jnp.maximum(base_max, jnp.max(candidates, axis=0))
    member_float = member.astype(jnp.float32)
    joint_at = jnp.dot(member_float, joint_max, precision=highest)
    rescale = jnp.exp(maxima - joint_at)
    base_rescale = jnp.exp(base_max - joint_max)
    scaled = (mixed_sum.reshape(slot_count, head_count, -1) * rescale[:, :, None]).reshape(
        slot_count, model_width
    )
    base_scaled = base_sum.reshape(img_count, head_count, -1) * base_rescale[:, :, None]
    collected = lax.dot_general(member_float, scaled, (((0,), (0,)), ((), ())), precision=highest)
    collected_total = lax.dot_general(
        member_float, totals * rescale, (((0,), (0,)), ((), ())), precision=highest
    )
    denominator = base_total * base_rescale + collected_total
    pooled = (base_scaled + collected.reshape(img_count, head_count, -1)) / denominator[:, :, None]
    return pooled.reshape(img_count, model_width).astype(jnp.bfloat16)


def unit_rows(matrix):
    return (matrix * lax.rsqrt(jnp.sum(matrix * matrix, axis=1, keepdims=True) + norm_eps)).astype(
        jnp.bfloat16
    )


def make_tile(image_rows, text_rows, row_labels, column_labels, scale_value, bias_value):
    logits = (
        scale_value
        * jnp.einsum("id,jd->ij", image_rows, text_rows, preferred_element_type=jnp.float32)
        + bias_value
    )
    target_sign = jnp.where(row_labels[:, None] == column_labels[None, :], 1.0, -1.0)
    return (scale_value * (-target_sign * jax.nn.sigmoid(-target_sign * logits))).astype(
        jnp.bfloat16
    )


def tile_terms(image_unit, text_block, block_labels, own_labels, scale_value, bias_value):
    grad_tile = make_tile(image_unit, text_block, own_labels, block_labels, scale_value, bias_value)
    image_term = jnp.dot(grad_tile, text_block, preferred_element_type=jnp.float32)
    text_term = jnp.einsum("ij,id->jd", grad_tile, image_unit, preferred_element_type=jnp.float32)
    return (image_term, text_term)


def per_device(
    crop_tokens,
    crop_lengths,
    crop_owner,
    crop_slot,
    base_tokens,
    key_probe,
    value_weight,
    out_weight,
    text_embed,
    pair_labels,
    logit_scale,
    logit_bias,
):
    owners = lax.axis_size("dp")
    crop_total = crop_tokens.shape[0]
    crop_width = crop_tokens.shape[1]
    model_width = crop_tokens.shape[2]
    img_count = base_tokens.shape[0]
    capacity = max(2, (2 * crop_total + owners - 1) // owners)
    slot_count = owners * capacity
    lengths = crop_lengths.reshape(-1)
    owner_ids = crop_owner[:, 0]
    member = (owner_ids[:, None] == lax.broadcasted_iota(jnp.int32, (1, owners), 1)).astype(
        jnp.int32
    )
    running = jnp.cumsum(member, axis=0)
    send_rank = jnp.sum(member * running, axis=1) - 1
    send_index = owner_ids * capacity + send_rank
    slot_ids = (
        jnp.zeros((slot_count,), jnp.int32).at[send_index].set(crop_slot).reshape(owners, capacity)
    )
    send_tokens = (
        jnp.zeros((slot_count, crop_width, model_width), jnp.bfloat16)
        .at[send_index]
        .set(crop_tokens)
    )
    send_lengths = jnp.zeros((slot_count,), jnp.int32).at[send_index].set(lengths)
    arrived_tokens = lax.all_to_all(
        send_tokens.reshape(owners, capacity, crop_width, model_width),
        "dp",
        split_axis=0,
        concat_axis=0,
        tiled=True,
    )
    arrived_lengths = lax.all_to_all(
        send_lengths.reshape(owners, capacity), "dp", split_axis=0, concat_axis=0, tiled=True
    )
    arrived_slots = lax.all_to_all(slot_ids, "dp", split_axis=0, concat_axis=0, tiled=True)
    mixed_sum, maxima, totals = crop_partial(
        arrived_tokens, arrived_lengths, key_probe, value_weight
    )
    received = (mixed_sum, maxima, totals, arrived_slots)
    flat_parts = tuple(
        (
            received_item.reshape((slot_count,) + received_item.shape[2:])
            for received_item in received
        )
    )
    base_lengths = jnp.full((img_count,), base_tokens.shape[1], jnp.int32)
    base_parts = crop_partial(base_tokens, base_lengths, key_probe, value_weight)
    pooled = merge_parts(base_parts, flat_parts, img_count)
    features = jnp.dot(pooled, out_weight, preferred_element_type=jnp.float32)
    image_embed = features.astype(jnp.bfloat16)
    image_unit = unit_rows(features)
    text_unit = unit_rows(text_embed.astype(jnp.float32))
    scale_value = logit_scale[0]
    bias_value = logit_bias[0]
    text_block = lax.all_gather(text_unit, "loop", axis=0, tiled=True)
    block_labels = lax.all_gather(pair_labels, "loop", axis=0, tiled=True)
    image_term, text_term = tile_terms(
        image_unit, text_block, block_labels, pair_labels, scale_value, bias_value
    )
    text_grad = lax.psum_scatter(
        text_term.astype(jnp.bfloat16), "loop", scatter_dimension=0, tiled=True
    ).astype(jnp.float32)
    return (image_embed, image_term, text_grad)


def solution(mesh):
    return jax.shard_map(
        per_device,
        mesh=mesh,
        in_specs=(
            P(("dp", "loop"), None, None),
            P(("dp", "loop"), None),
            P(("dp", "loop"), None),
            P(("dp", "loop")),
            P(("dp", "loop"), None, None),
            P(),
            P(),
            P(),
            P(("dp", "loop"), None),
            P(("dp", "loop")),
            P(),
            P(),
        ),
        out_specs=(P(("dp", "loop"), None), P(("dp", "loop"), None), P(("dp", "loop"), None)),
        check_vma=False,
    )
```

profile of v0, /device:TPU:0, one launch (start us, length us, event | category | flops | bytes accessed | tf_op | source)
XLA Modules:
  0.0 538.3 jit_solution(3503626312159067026)
XLA Ops:
  7.2 0.9 fusion.41
  8.2 0.8 select_reduce_fusion.1
  9.0 0.7 fusion.48
  9.7 0.9 scatter_custom_fusion.1
  10.6 0.7 all_to_all.17
  11.3 6.5 %all-to-all-start.1 = ((s32[16,1,8]{2,1,0:T(1,128)}), s32[16,1,8]{2,1,0:T(1,128)S(1)}, u32[]{:S(2)}, u32[]{:S(2)}) async-start(s32[16,1,8]{2,1,0:T(1,128)} %bitcast.8), calls=%async_computation.1 | async-start | bytes 16384 | tf_op jit(solution)/shard_map/all_to_all | solution.py:129
  17.7 0.9 scatter_custom_fusion
  18.6 0.7 all_to_all.15
  19.3 4.4 all-to-all-done.1
  23.7 3.5 all-to-all-start
  27.2 7.2 %broadcast_in_dim.92 = bf16[128,64,1152]{2,1,0:T(8,128)(2,1)} broadcast(bf16[]{:T(256)} %constant.10.clone.1), dimensions={} | broadcast | bytes 18874370 | tf_op jit(solution)/shard_map/broadcast_in_dim | solution.py:117
  34.4 23.4 %scatter_fusion = bf16[128,64,1152]{2,1,0:T(8,128)(2,1)} fusion(bf16[128,64,1152]{2,1,0:T(8,128)(2,1)} %broadcast_in_dim.92, s32[64]{0:T(128)S(1)} %fusion.48, bf16[64,64,1152]{2,1,0:T(8,128)(2,1)} %param.12), kind=kCustom, calls=%fused_computation.2 | custom fusion | bytes 28311808 | tf_op jit(solution)/shard_map/scatter | solution.py:119
  57.8 5.9 %all-to-all-start.2 = ((bf16[16,8,64,1152]{3,2,1,0:T(8,128)(2,1)}), bf16[16,8,64,1152]{3,2,1,0:T(8,128)(2,1)}, u32[]{:S(2)}, u32[]{:S(2)}) async-start(bf16[16,8,64,1152]{3,2,1,0:T(8,128)(2,1)} %bitcast.60), calls=%async_computation.2 | async-start | bytes 37748736 | tf_op jit(solution)/shard_map/all_to_all | solution.py:122
  63.8 2.4 convolution_multiply_fusion.1
  66.3 0.3 fusion.32
  66.6 0.2 copy-done.5
  66.8 0.3 fusion.33
  67.2 5.3 copy.67
  73.8 0.6 dynamic-slice
  75.1 0.2 dynamic-update-slice
  75.3 285.2 %all-reduce = s32[256]{0:T(256)} all-reduce(s32[256]{0:T(256)S(1)} %dynamic-update-slice), channel_id=1, replica_groups=mesh['dp'=16,'loop'=8] {'loop'}, use_global_device_ids=true, to_apply=%add | all-reduce | flops 256 | bytes 2048
  360.7 35.4 %all_gather.7 = bf16[256,1152]{1,0:T(8,128)(2,1)S(1)} all-gather(bf16[32,1152]{1,0:T(8,128)(2,1)S(1)} %fusion.36), channel_id=1, replica_groups=mesh['dp'=16,'loop'=8] {'loop'}, dimensions={0}, use_global_device_ids=true | all-gather | bytes 663552 | tf_op jit(solution)/shard_map/all_gather | solution.py:152
  396.1 4.5 fusion.34
  400.5 0.5 broadcast.92
  401.1 0.7 reduce.3
  401.9 12.1 %convolution_multiply_fusion = f32[8192,16]{0,1:T(8,128)} fusion(bf16[8192,1152]{1,0:T(8,128)(2,1)} %bitcast.11, bf16[1152,16]{0,1:T(8,128)(2,1)} %param.17), kind=kOutput, calls=%fused_computation.5 | convolution fusion | flops 302120960 | bytes 19435520 | tf_op jit(solution)/shard_map/dot_general | solution.py:20
  414.1 2.4 reshape.119
  416.5 2.0 fusion.25
  418.6 0.2 select_reduce_fusion
  418.8 0.1 fusion.24
  419.0 2.4 fusion.26
  421.4 0.9 mul.78
  422.3 2.1 copy.81
  424.4 12.4 %fusion.27 = f32[16,8,16,1152]{3,2,1,0:T(8,128)S(1)} fusion(bf16[16,8,64,1152]{3,2,1,0:T(8,128)(2,1)} %all-to-all-done.2, f32[16,8,64,16]{2,1,0,3:T(8,128)} %reshape.119, f32[16,8,16]{2,1,0:T(8,128)S(1)} %fusion.25, pred[16,8,64]{2,1,0:T(8,128)(4,1)S(1)} %iota_compare_fusion), kind=kOutput, calls=%fused_computation.33 | convolution fusion | flops 1812332544 | bytes 28852224 | tf_op jit(solution)/shard_map/...kh,...kd->...hd/dot_general | solution.py:28
  436.9 7.0 %fusion.4 = f32[16,8,16,72]{3,1,0,2:T(8,128)S(1)} fusion(bf16[1152,16,72,1]{0,2,3,1:T(8,128)(2,1)S(1)} %bitcast.62, f32[16,8,16,1152]{3,2,1,0:T(8,128)S(1)} %fusion.27), kind=kOutput, calls=%fused_computation.9 | convolution fusion | flops 2038431744 | bytes 12681216 | tf_op jit(solution)/shard_map/...hd,dhe->...he/dot_general | solution.py:30
  443.8 1.6 copy.79
  445.4 2.4 reshape_reshape_reshape.3
  447.9 2.1 multiply_bitcast_fusion
  450.0 2.1 copy.82
  452.2 5.3 fusion.10
  457.6 0.9 fusion.14
  458.5 0.2 convert_element_type.37
  458.7 1.3 multiply_reduce_fusion
  460.0 0.3 fusion.23
  460.4 1.2 convolution_convert_fusion
  461.6 0.9 fusion.57
  462.4 67.5 %reduce-scatter.2.cloned.1.call-done = bf16[32,1152]{1,0:T(8,128)(2,1)} async-done(((bf16[256,1152]{1,0:T(8,128)(2,1)}), bf16[32,1152]{1,0:T(8,128)(2,1)}) %reduce-scatter.2.cloned.1.call-update) | async-done | bytes 73744 | tf_op jit(solution)/shard_map/reduce_scatter | solution.py:157
  529.9 1.6 convert_element_type.44
  (42 shorter events, 1.2 us)
Async XLA Ops:
  7.2 451.5 %copy-start = (bf16[1152,1152]{1,0:T(8,128)(2,1)S(1)}, bf16[1152,1152]{1,0:T(8,128)(2,1)}, u32[]{:S(2)}) copy-start(bf16[1152,1152]{1,0:T(8,128)(2,1)} %param.19) | copy-start | bytes 7962628
  11.3 12.5 %all-to-all-start.1 = ((s32[16,1,8]{2,1,0:T(1,128)}), s32[16,1,8]{2,1,0:T(1,128)S(1)}, u32[]{:S(2)}, u32[]{:S(2)}) async-start(s32[16,1,8]{2,1,0:T(1,128)} %bitcast.8), calls=%async_computation.1 | async-start | bytes 16384 | tf_op jit(solution)/shard_map/all_to_all | solution.py:129
  23.7 34.0 %all-to-all-start = ((s32[16,1,8]{2,1,0:T(1,128)}), s32[16,1,8]{2,1,0:T(1,128)S(1)}, u32[]{:S(2)}, u32[]{:S(2)}) async-start(s32[16,1,8]{2,1,0:T(1,128)} %bitcast.6), calls=%async_computation | async-start | bytes 16384 | tf_op jit(solution)/shard_map/all_to_all | solution.py:132
  57.8 6.0 %copy-start.4 = (bf16[1152,16]{0,1:T(8,128)(2,1)S(1)}, bf16[1152,16]{0,1:T(8,128)(2,1)}, u32[]{:S(2)}) copy-start(bf16[1152,16]{0,1:T(8,128)(2,1)} %param.17) | copy-start | bytes 110596
  57.8 344.2 %all-to-all-start.2 = ((bf16[16,8,64,1152]{3,2,1,0:T(8,128)(2,1)}), bf16[16,8,64,1152]{3,2,1,0:T(8,128)(2,1)}, u32[]{:S(2)}, u32[]{:S(2)}) async-start(bf16[16,8,64,1152]{3,2,1,0:T(8,128)(2,1)} %bitcast.60), calls=%async_computation.2 | async-start | bytes 37748736 | tf_op jit(solution)/shard_map/all_to_all | solution.py:122
  63.7 466.2 %reduce-scatter.2.cloned.1.call-start = ((), (), s32[]{:S(2)}) async-start(), calls=%async_computation.4 | async-start | bytes 663552 | tf_op jit(solution)/shard_map/reduce_scatter | solution.py:157
  66.3 0.5 copy-start.5
  67.1 6.6 %copy-start.9 = (u32[128]{0:T(128)S(1)}, u32[128]{0:T(128)}, u32[]{:S(2)}) copy-start(u32[128]{0:T(128)} %constant.46) | copy-start | bytes 1540
  67.2 7.9 %copy-start.7 = (s32[32]{0:T(128)S(1)}, s32[32]{0:T(128)}, u32[]{:S(2)}) copy-start(s32[32]{0:T(128)} %param.21) | copy-start | bytes 388
  67.2 293.3 %copy-start.3 = (bf16[32,1152]{1,0:T(8,128)(2,1)S(1)}, bf16[32,1152]{1,0:T(8,128)(2,1)}, u32[]{:S(2)}) copy-start(bf16[32,1152]{1,0:T(8,128)(2,1)} %param.20) | copy-start | bytes 221188
  424.4 12.5 %copy-start.1 = (bf16[1152,1152]{0,1:T(8,128)(2,1)S(1)}, bf16[1152,1152]{0,1:T(8,128)(2,1)}, u32[]{:S(2)}) copy-start(bf16[1152,1152]{0,1:T(8,128)(2,1)} %copy.67) | copy-start | bytes 7962628
  452.2 5.4 copy-start.2
  457.5 2.5 copy-start.6
  457.6 2.5 copy-start.8
Sparse Core Ops, SparseCore 0:
  461.7 68.1 reduce-scatter.1
where the time goes:
time: 540 us; the launch traced here: 538 us
  blocking collectives  321 us (59%)
  waiting for transfers between devices  71.9 us (13%)
  local copies, waits for them, and re-layouts  52.9 us (10%)
  matrix products  48.5 us (9%)
  between operations  16.3 us (3%)
  starting transfers between devices  15.9 us (3%)
  other arithmetic  12.2 us (2%)
    unnamed x1, blocking collectives  285 us
    reduce_scatter x1, waiting for transfers between devices, per_device(): lax.psum_scatter(text_term.astype(jnp.bfloat16), 'loop', scatter_dimensio...  67.5 us
    all_gather x1, blocking collectives, per_device(): text_block = lax.all_gather(text_unit, 'loop', axis=0, tiled=True)  35.4 us
    scatter x1, local copies, waits for them, and re-layouts, per_device(): send_tokens = jnp.zeros((slot_count, crop_width, model_width), jnp.bfloat...  23.4 us
    dot_general x2, matrix products, crop_partial(): jnp.einsum('...kh,...kd->...hd', weight, tokens.astype(jnp.float32), prec...  16.9 us
    dot_general x2, matrix products, crop_partial(): jnp.dot(flat_rows, key_probe, preferred_element_type=jnp.float32)  14.5 us
    dot_general x2, matrix products, crop_partial(): jnp.einsum('...hd,dhe->...he', mixed, value_heads, precision=highest)  12.3 us
  transfers between devices with their start and end apart: 4, of which 2 were waited for; matrix products, arithmetic and copies ran while one was open for 9% of the time, Pallas kernels for 0%

commit v1 on v0

v1 whole, which is shorter than its diff:
```python
import math

import jax
import jax.numpy as jnp
from jax import lax
from jax.experimental import pallas as pl
from jax.experimental.pallas import tpu as pltpu
from jax.sharding import PartitionSpec as P

very_low = -1e30
norm_eps = 1e-06
highest = lax.Precision.HIGHEST
f32 = jnp.float32
bf16 = jnp.bfloat16
contract_last = (((1,), (1,)), ((), ()))
lanes = 128
col_tile = 256


def iota(shape, dim):
    return lax.broadcasted_iota(jnp.int32, shape, dim)


def column_tiles(width, head_dim):
    tiles = []
    for low in range(0, width, col_tile):
        high = min(low + col_tile, width)
        tiles.append((low, high, low // head_dim, (high - 1) // head_dim))
    return tiles


def own_head(shape, low, head, head_dim):
    column = iota(shape, 1) + low
    return (column >= head * head_dim) & (column < (head + 1) * head_dim)


def gather_heads(mixed_ref, rows_ref, count, heads):
    for part in range(rows_ref.shape[1] // lanes):
        for head in range(heads):
            rows_ref[head * count : (head + 1) * count, part * lanes : (part + 1) * lanes] = (
                mixed_ref[pl.ds(part * count * heads + head, count, stride=heads), :].astype(bf16)
            )


def project_heads(rows_ref, value_ref, count, low, high, first, last, head_dim):
    stacked = jnp.dot(
        rows_ref[first * count : (last + 1) * count, :],
        value_ref[:, low:high],
        preferred_element_type=f32,
    )
    total = jnp.zeros((count, high - low), f32)
    for head in range(first, last + 1):
        part = stacked[(head - first) * count : (head - first + 1) * count, :]
        total = jnp.where(own_head(part.shape, low, head, head_dim), part, total)
    return total


def crop_kernel(
    length_ref,
    token_ref,
    probe_ref,
    owner_ref,
    slot_ref,
    value_hbm,
    send_ref,
    probe_rows,
    maxima_ref,
    total_ref,
    mixed_ref,
    rows_ref,
    value_ref,
    value_sem,
    *,
    capacity,
):
    step = pl.program_id(0)
    block, width, model = token_ref.shape
    heads = probe_ref.shape[1]
    head_dim = model // heads
    crops = owner_ref.shape[1]
    slots = send_ref.shape[0]
    value_copy = pltpu.make_async_copy(value_hbm, value_ref, value_sem)

    @pl.when(step == 0)
    def _():
        value_copy.start()
        probe_rows[...] = probe_ref[...].astype(f32).T.astype(bf16)
        maxima_ref[...] = jnp.zeros(maxima_ref.shape, f32)
        total_ref[...] = jnp.zeros(total_ref.shape, f32)

    tokens = token_ref[...].reshape(block * width, model)
    scores = lax.dot_general(
        probe_rows[...], tokens, contract_last, preferred_element_type=f32
    ) * (1.0 / math.sqrt(head_dim))
    per_group = lanes // width
    lane = iota((heads, lanes), 1)
    maxima = maxima_ref[...]
    totals = total_ref[...]
    weights = []
    for local in range(block):
        group, place = divmod(local, per_group)
        crop = step * block + local
        part = scores[:, group * lanes : (group + 1) * lanes]
        valid = (lane >= place * width) & (lane < place * width + length_ref[0, crop])
        masked = jnp.where(valid, part, very_low)
        peak = jnp.max(masked, axis=1, keepdims=True).astype(bf16).astype(f32)
        weight = jnp.where(valid, jnp.exp(masked - peak), 0.0).astype(bf16)
        amount = jnp.sum(weight.astype(f32), axis=1, keepdims=True)
        maxima = jnp.where(lane == crop, peak, maxima)
        totals = jnp.where(lane == crop, amount, totals)
        weights.append(weight)
    maxima_ref[...] = maxima
    total_ref[...] = totals
    quad = 2 * per_group
    empty = jnp.zeros((heads, lanes), bf16)
    for first in range(0, block, quad):
        rows = [
            jnp.concatenate(
                [weights[first + k], empty] if k < per_group else [empty, weights[first + k]],
                axis=1,
            )
            for k in range(quad)
        ]
        base = pl.multiple_of(step * (block * heads), block * heads) + first * heads
        mixed = jnp.dot(
            jnp.concatenate(rows, axis=0),
            tokens[first * width : (first + quad) * width, :],
            preferred_element_type=f32,
        )
        for part in range(model // lanes):
            mixed_ref[pl.ds(part * crops * heads + base, quad * heads), :] = mixed[
                :, part * lanes : (part + 1) * lanes
            ]

    @pl.when(step == pl.num_programs(0) - 1)
    def _():
        gather_heads(mixed_ref, rows_ref, crops, heads)
        square = (crops, crops)
        owner_row = owner_ref[...]
        owner_column = jnp.sum(
            jnp.where(iota(square, 0) == iota(square, 1), owner_row, 0), axis=1, keepdims=True
        )
        earlier = (owner_column == owner_row) & (iota(square, 0) < iota(square, 1))
        rank = jnp.sum(earlier.astype(jnp.int32), axis=0, keepdims=True)
        place = owner_row * capacity + rank
        member = (iota((slots, crops), 0) == place).astype(bf16)
        total = total_ref[:, :crops]
        coarse = total.astype(bf16).astype(f32)
        row = iota((lanes - 3 * heads, crops), 0)
        extra = jnp.where(
            row == 0, slot_ref[...].astype(f32), jnp.where(row == 1, 1.0, 0.0)
        )
        meta = jnp.concatenate([maxima_ref[:, :crops], coarse, total - coarse, extra], axis=0)
        send_ref[:, model:] = lax.dot_general(
            member, meta.astype(bf16), contract_last, preferred_element_type=f32
        ).astype(bf16)
        value_copy.wait()
        for low, high, first, last in column_tiles(model, head_dim):
            summed = project_heads(rows_ref, value_ref, crops, low, high, first, last, head_dim)
            send_ref[:, low:high] = jnp.dot(
                member, summed.astype(bf16), preferred_element_type=f32
            ).astype(bf16)


def base_kernel(
    token_ref, probe_ref, value_ref, sum_ref, maxima_ref, total_ref, mixed_ref, rows_ref
):
    count, width, model = token_ref.shape
    heads = probe_ref.shape[1]
    head_dim = model // heads
    probe_rows = probe_ref[...].astype(f32).T.astype(bf16)
    per_group = lanes // width
    octet = 2 * per_group
    lane = iota((heads, lanes), 1)
    maxima = jnp.zeros((heads, lanes), f32)
    totals = jnp.zeros((heads, lanes), f32)
    empty = jnp.zeros((heads, lanes), bf16)
    for start in range(0, count, octet):
        tokens = token_ref[start : start + octet].reshape(octet * width, model)
        scores = lax.dot_general(
            probe_rows, tokens, contract_last, preferred_element_type=f32
        ) * (1.0 / math.sqrt(head_dim))
        rows = []
        for local in range(octet):
            group, place = divmod(local, per_group)
            part = scores[:, group * lanes : (group + 1) * lanes]
            valid = (lane >= place * width) & (lane < (place + 1) * width)
            masked = jnp.where(valid, part, very_low)
            peak = jnp.max(masked, axis=1, keepdims=True)
            weight = jnp.where(valid, jnp.exp(masked - peak), 0.0).astype(bf16)
            amount = jnp.sum(weight.astype(f32), axis=1, keepdims=True)
            maxima = jnp.where(lane == start + local, peak, maxima)
            totals = jnp.where(lane == start + local, amount, totals)
            rows.append(
                jnp.concatenate([weight, empty] if group == 0 else [empty, weight], axis=1)
            )
        mixed = jnp.dot(jnp.concatenate(rows, axis=0), tokens, preferred_element_type=f32)
        for part in range(model // lanes):
            base = part * count * heads + start * heads
            mixed_ref[base : base + octet * heads, :] = mixed[:, part * lanes : (part + 1) * lanes]
    maxima_ref[...] = maxima
    total_ref[...] = totals
    gather_heads(mixed_ref, rows_ref, count, heads)
    for low, high, first, last in column_tiles(model, head_dim):
        sum_ref[:, low:high] = project_heads(
            rows_ref, value_ref, count, low, high, first, last, head_dim
        )


def merge_kernel(
    arrived_ref,
    base_ref,
    base_max_ref,
    base_total_ref,
    text_ref,
    label_ref,
    out_weight_hbm,
    embed_ref,
    spread_ref,
    pooled_ref,
    out_weight_ref,
    weight_sem,
):
    count, model = base_ref.shape
    heads = base_max_ref.shape[0]
    head_dim = model // heads
    slots = arrived_ref.shape[0]
    weight_copy = pltpu.make_async_copy(out_weight_hbm, out_weight_ref, weight_sem)
    weight_copy.start()
    square = (lanes, lanes)
    identity = (iota(square, 0) == iota(square, 1)).astype(bf16)
    meta = lax.dot_general(
        identity, arrived_ref[:, model:], contract_last, preferred_element_type=f32
    )
    maxima = meta[:heads]
    totals = meta[heads : 2 * heads] + meta[2 * heads : 3 * heads]
    slot_row = meta[3 * heads : 3 * heads + 1]
    present = meta[3 * heads + 1 : 3 * heads + 2] > 0.5
    base_max = base_max_ref[...]
    lane = iota((heads, lanes), 1)
    joint = jnp.zeros((heads, lanes), f32)
    joint_at = jnp.zeros((heads, slots), f32)
    for image in range(count):
        mine = present & (slot_row == float(image))
        peak = jnp.maximum(
            jnp.max(jnp.where(mine, maxima, very_low), axis=1, keepdims=True),
            base_max[:, image : image + 1],
        )
        joint = jnp.where(lane == image, peak, joint)
        joint_at = jnp.where(mine, peak, joint_at)
    rescale = jnp.where(present, jnp.exp(maxima - joint_at), 0.0).astype(bf16).astype(f32)
    base_rescale = jnp.exp(base_max - joint)
    member = (
        present & (slot_row == iota((count, slots), 0).astype(f32))
    ).astype(f32)
    base_part = jnp.concatenate(
        [base_rescale, base_total_ref[...] * base_rescale, jnp.zeros((lanes - 2 * heads, lanes), f32)],
        axis=0,
    ).T
    base_scale = base_part[:count, :heads]
    denominator = base_part[:count, heads : 2 * heads] + lax.dot_general(
        member, totals * rescale, contract_last, preferred_element_type=f32, precision=highest
    )
    inverse = 1.0 / denominator
    for low, high, first, last in column_tiles(model, head_dim):
        stacked = jnp.dot(
            jnp.concatenate(
                [
                    (member * rescale[head : head + 1, :]).astype(bf16)
                    for head in range(first, last + 1)
                ],
                axis=0,
            ),
            arrived_ref[:, low:high],
            preferred_element_type=f32,
        )
        base_tile = base_ref[:, low:high]
        pooled = jnp.zeros((count, high - low), f32)
        for head in range(first, last + 1):
            part = stacked[(head - first) * count : (head - first + 1) * count, :]
            part = (part + base_tile * base_scale[:, head : head + 1]) * inverse[:, head : head + 1]
            pooled = jnp.where(own_head(part.shape, low, head, head_dim), part, pooled)
        pooled_ref[:, low:high] = pooled.astype(bf16)
    text = text_ref[...].astype(f32)
    text_unit = (
        text * lax.rsqrt(jnp.sum(text * text, axis=1, keepdims=True) + norm_eps)
    ).astype(bf16)
    own = (count, count)
    label_column = jnp.sum(
        jnp.where(iota(own, 0) == iota(own, 1), label_ref[...], 0), axis=1, keepdims=True
    )
    label_lanes = jnp.broadcast_to(label_column.astype(f32), (count, lanes)).astype(bf16)
    weight_copy.wait()
    features = jnp.dot(pooled_ref[...], out_weight_ref[...], preferred_element_type=f32)
    embed_ref[...] = features.astype(bf16)
    image_unit = (
        features * lax.rsqrt(jnp.sum(features * features, axis=1, keepdims=True) + norm_eps)
    ).astype(bf16)
    for peer in range(spread_ref.shape[0]):
        spread_ref[peer, :count, :model] = image_unit
        spread_ref[peer, :count, model:] = jnp.zeros((count, lanes), bf16)
        spread_ref[peer, count:, :model] = text_unit
        spread_ref[peer, count:, model:] = label_lanes


def grad_kernel(
    scale_ref, bias_ref, gathered_ref, own_ref, image_grad_ref, text_grad_ref, image_all, text_all
):
    peers, double, padded = gathered_ref.shape
    count = double // 2
    model = padded - lanes
    labels = []
    for peer in range(peers):
        image_all[peer * count : (peer + 1) * count, :] = gathered_ref[peer, :count, :model]
        text_all[peer * count : (peer + 1) * count, :] = gathered_ref[peer, count:, :model]
        labels.append(gathered_ref[peer, count:, model:])
    first_lane = (iota((8, lanes), 1) == 0).astype(bf16)
    label_row = lax.dot_general(
        first_lane, jnp.concatenate(labels, axis=0), contract_last, preferred_element_type=f32
    )[:1]
    label_column = own_ref[0, count:, model : model + 1].astype(f32)
    scale = scale_ref[0]
    bias = bias_ref[0]
    sign = jnp.where(label_column == label_row, 1.0, -1.0)

    def one_side(own_rows, all_rows, other_rows):
        logits = scale * lax.dot_general(
            own_rows, all_rows[...], contract_last, preferred_element_type=f32
        ) + bias
        tile = (scale * (-sign * jax.nn.sigmoid(-sign * logits))).astype(bf16)
        return jnp.dot(tile, other_rows[...], preferred_element_type=f32)

    image_grad_ref[...] = one_side(own_ref[0, :count, :model], text_all, text_all)
    text_grad_ref[...] = one_side(own_ref[0, count:, :model], image_all, image_all)


def per_device(
    crop_tokens,
    crop_lengths,
    crop_owner,
    crop_slot,
    base_tokens,
    key_probe,
    value_weight,
    out_weight,
    text_embed,
    pair_labels,
    logit_scale,
    logit_bias,
):
    owners = lax.axis_size("dp")
    peers = lax.axis_size("loop")
    crops, width, model = crop_tokens.shape
    count = base_tokens.shape[0]
    heads = key_probe.shape[1]
    capacity = max(2, (2 * crops + owners - 1) // owners)
    slots = owners * capacity
    padded = model + lanes
    block = 8
    vmem = pl.BlockSpec(memory_space=pltpu.VMEM)
    smem = pl.BlockSpec(memory_space=pltpu.SMEM)
    anywhere = pl.BlockSpec(memory_space=pl.ANY)
    whole = lambda *shape: pl.BlockSpec(shape, lambda step, lengths: (0,) * len(shape))

    def crop_body(*refs):
        crop_kernel(*refs, capacity=capacity)

    send = pl.pallas_call(
        crop_body,
        grid_spec=pltpu.PrefetchScalarGridSpec(
            num_scalar_prefetch=1,
            grid=(crops // block,),
            in_specs=[
                pl.BlockSpec((block, width, model), lambda step, lengths: (step, 0, 0)),
                whole(model, heads),
                whole(1, crops),
                whole(1, crops),
                anywhere,
            ],
            out_specs=whole(slots, padded),
            scratch_shapes=[
                pltpu.VMEM((heads, model), bf16),
                pltpu.VMEM((heads, lanes), f32),
                pltpu.VMEM((heads, lanes), f32),
                pltpu.VMEM((model // lanes * crops * heads, lanes), f32),
                pltpu.VMEM((crops * heads, model), bf16),
                pltpu.VMEM((model, model), bf16),
                pltpu.SemaphoreType.DMA,
            ],
        ),
        out_shape=jax.ShapeDtypeStruct((slots, padded), bf16),
        name="crop_partial",
    )(
        crop_lengths,
        crop_tokens,
        key_probe,
        crop_owner.reshape(1, crops),
        crop_slot.reshape(1, crops),
        value_weight,
    )
    arrived = lax.all_to_all(send, "dp", split_axis=0, concat_axis=0, tiled=True)
    base_sum, base_max, base_total = pl.pallas_call(
        base_kernel,
        in_specs=[vmem] * 3,
        out_specs=[vmem] * 3,
        out_shape=[
            jax.ShapeDtypeStruct((count, model), f32),
            jax.ShapeDtypeStruct((heads, lanes), f32),
            jax.ShapeDtypeStruct((heads, lanes), f32),
        ],
        scratch_shapes=[
            pltpu.VMEM((model // lanes * count * heads, lanes), f32),
            pltpu.VMEM((count * heads, model), bf16),
        ],
        name="base_partial",
    )(base_tokens, key_probe, value_weight)
    image_embed, spread = pl.pallas_call(
        merge_kernel,
        in_specs=[vmem] * 6 + [anywhere],
        out_specs=[vmem] * 2,
        out_shape=[
            jax.ShapeDtypeStruct((count, model), bf16),
            jax.ShapeDtypeStruct((peers, 2 * count, padded), bf16),
        ],
        scratch_shapes=[
            pltpu.VMEM((count, model), bf16),
            pltpu.VMEM((model, model), bf16),
            pltpu.SemaphoreType.DMA,
        ],
        name="merge_parts",
    )(
        arrived,
        base_sum,
        base_max,
        base_total,
        text_embed,
        pair_labels.reshape(1, count),
        out_weight,
    )
    gathered = lax.all_to_all(spread, "loop", split_axis=0, concat_axis=0, tiled=True)
    image_grad, text_grad = pl.pallas_call(
        grad_kernel,
        in_specs=[smem, smem, vmem, vmem],
        out_specs=[vmem] * 2,
        out_shape=[
            jax.ShapeDtypeStruct((count, model), f32),
            jax.ShapeDtypeStruct((count, model), f32),
        ],
        scratch_shapes=[
            pltpu.VMEM((peers * count, model), bf16),
            pltpu.VMEM((peers * count, model), bf16),
        ],
        name="loss_grads",
    )(logit_scale, logit_bias, gathered, spread)
    return (image_embed, image_grad, text_grad)


def solution(mesh):
    return jax.shard_map(
        per_device,
        mesh=mesh,
        in_specs=(
            P(("dp", "loop"), None, None),
            P(("dp", "loop"), None),
            P(("dp", "loop"), None),
            P(("dp", "loop")),
            P(("dp", "loop"), None, None),
            P(),
            P(),
            P(),
            P(("dp", "loop"), None),
            P(("dp", "loop")),
            P(),
            P(),
        ),
        out_specs=(P(("dp", "loop"), None), P(("dp", "loop"), None), P(("dp", "loop"), None)),
        check_vma=False,
    )
```

time: 540 us -> 69.2 us (0.13)
  blocking collectives: 321 us -> 0 us
  waiting for transfers between devices: 71.9 us -> 18.6 us
  local copies, waits for them, and re-layouts: 52.9 us -> 3.46 us
  matrix products: 48.5 us -> 0 us
  Pallas kernels: 0 us -> 31.5 us
  between operations: 16.3 us -> 1.96 us
  other arithmetic: 12.2 us -> 0 us
    unnamed x1 -> x0, blocking collectives: 285 us -> none
    reduce_scatter x1 -> x0, waiting for transfers between devices: 67.5 us -> none  [per_device(): lax.psum_scatter(text_term.astype(jnp.bfloat16), 'loop', scatter_dimensio...]
    dot_general x13 -> x0, matrix products: 48.5 us -> none  [the longest x2 16.9 us: crop_partial(): jnp.einsum('...kh,...kd->...hd', weight, tokens.astype(jnp.float32), prec...]
    all_gather x1 -> x0, blocking collectives: 35.4 us -> none  [per_device(): text_block = lax.all_gather(text_unit, 'loop', axis=0, tiled=True)]
    pallas_call x0 -> x4, Pallas kernels: none -> 31.5 us  [the longest x1 15.3 us: per_device(): pl.pallas_call(crop_body, grid_spec=pltpu.PrefetchScalarGridSpec(num_scal...]
    scatter x3 -> x0, local copies, waits for them, and re-layouts: 25.2 us -> none  [the longest x1 23.4 us: per_device(): send_tokens = jnp.zeros((slot_count, crop_width, model_width), jnp.bfloat...]
    all_to_all x3 -> x2, waiting for transfers between devices: 4.41 us -> 18.6 us  [the longest x1 16.5 us: per_device(): lax.all_to_all(spread, 'loop', split_axis=0, concat_axis=0, tiled=True)]
    broadcast_in_dim x2 -> x0, local copies, waits for them, and re-layouts: 7.22 us -> none  [the longest x1 7.17 us: per_device(): jnp.zeros((slot_count, crop_width, model_width), jnp.bfloat16)]
  transfers between devices with their start and end apart: 4 -> 2, of which waited for: 2 -> 2; matrix products, arithmetic and copies ran while one was open for 9% -> 0% of each run, Pallas kernels for 0% -> 10%
where the time goes in v1:
time: 69.2 us; the launch traced here: 68.6 us
  Pallas kernels  31.5 us (46%)
  waiting for transfers between devices  18.6 us (27%)
  starting transfers between devices  13.1 us (19%)
  local copies, waits for them, and re-layouts  3.46 us (5%)
  between operations  1.96 us (3%)
    all_to_all x1, waiting for transfers between devices, per_device(): lax.all_to_all(spread, 'loop', split_axis=0, concat_axis=0, tiled=True)  16.5 us
    pallas_call x1, Pallas kernels, per_device(): pl.pallas_call(crop_body, grid_spec=pltpu.PrefetchScalarGridSpec(num_scal...  15.3 us
    all_to_all x1, starting transfers between devices, per_device(): lax.all_to_all(spread, 'loop', split_axis=0, concat_axis=0, tiled=True)  6.65 us
    pallas_call x1, Pallas kernels, per_device(): pl.pallas_call(base_kernel, in_specs=[vmem] * 3, out_specs=[vmem] * 3, ou...  6.63 us
    all_to_all x1, starting transfers between devices, per_device(): lax.all_to_all(send, 'dp', split_axis=0, concat_axis=0, tiled=True)  6.47 us
    pallas_call x1, Pallas kernels, per_device(): pl.pallas_call(merge_kernel, in_specs=[vmem] * 6 + [anywhere], out_specs=...  6 us
    pallas_call x1, Pallas kernels, per_device(): pl.pallas_call(grad_kernel, in_specs=[smem, smem, vmem, vmem], out_specs=...  3.59 us
    unnamed x5, local copies, waits for them, and re-layouts  3.46 us
  transfers between devices with their start and end apart: 2, of which 2 were waited for; matrix products, arithmetic and copies ran while one was open for 0% of the time, Pallas kernels for 10%

profile of v1, /device:TPU:0, one launch (start us, length us, event | category | flops | bytes accessed | tf_op | source)
XLA Modules:
  0.0 68.6 jit_solution(1128800763203054121)
XLA Ops:
  0.6 1.7 %copy.15.refs_2_.probe_ref = bf16[1152,16]{1,0:T(8,128)(2,1)} copy(bf16[1152,16]{0,1:T(8,128)(2,1)} %param.17) | data formatting | bytes 73728 | tf_op args[5]
  2.3 15.3 %crop_partial.1 = bf16[128,1280]{1,0:T(8,128)(2,1)} custom-call(s32[1,64]{1,0:T(1,128)} %refs_0_.1, bf16[64,64,1152]{2,1,0:T(8,128)(2,1)} %refs_1_.1, bf16[1152,16]{1,0:T(8,128)(2,1)} %copy.15.refs_2_.probe_ref, s32[1,64]{1,0:T(1,128)} %bitcast.7, s32[1,64]{1,0:T(1,128)} %bitcast.8, bf16[1152,1152]{1,0:T(8,128)(2,1)} %value_ref.1), custom_call_target="tpu_custom_call" | custom-call | tf_op jit(solution)/shard_map/crop_partial/pallas_call | solution.py:368
  17.6 6.5 %all-to-all-start = ((bf16[16,8,1280]{2,1,0:T(8,128)(2,1)}), bf16[16,8,1280]{2,1,0:T(8,128)(2,1)S(1)}, u32[]{:S(2)}, u32[]{:S(2)}) async-start(bf16[16,8,1280]{2,1,0:T(8,128)(2,1)} %bitcast.5), calls=%async_computation | async-start | bytes 655360 | tf_op jit(solution)/shard_map/all_to_all | solution.py:401
  24.0 6.6 %base_partial.1 = (f32[32,1152]{1,0:T(8,128)}, f32[16,128]{1,0:T(8,128)}, f32[16,128]{1,0:T(8,128)}) custom-call(bf16[32,32,1152]{2,1,0:T(8,128)(2,1)} %token_ref.1, bf16[1152,16]{1,0:T(8,128)(2,1)} %copy.15.refs_2_.probe_ref, bf16[1152,1152]{1,0:T(8,128)(2,1)} %value_ref.1), custom_call_target="tpu_custom_call" | custom-call | tf_op jit(solution)/shard_map/base_partial/pallas_call | solution.py:402
  30.7 2.1 %all-to-all-done = bf16[16,8,1280]{2,1,0:T(8,128)(2,1)S(1)} async-done(((bf16[16,8,1280]{2,1,0:T(8,128)(2,1)}), bf16[16,8,1280]{2,1,0:T(8,128)(2,1)S(1)}, u32[]{:S(2)}, u32[]{:S(2)}) %all-to-all-start) | async-done | bytes 327712 | tf_op jit(solution)/shard_map/all_to_all | solution.py:401
  32.8 0.0 copy-start.1
  32.8 0.7 %copy-done.1 = bf16[16,8,1280]{2,1,0:T(8,128)(2,1)} copy-done((bf16[16,8,1280]{2,1,0:T(8,128)(2,1)}, bf16[16,8,1280]{2,1,0:T(8,128)(2,1)S(1)}, u32[]{:S(2)}) %copy-start.1) | copy-done | bytes 327704
  33.5 6.0 %merge_parts.1 = (bf16[32,1152]{1,0:T(8,128)(2,1)}, bf16[8,64,1280]{2,1,0:T(8,128)(2,1)}) custom-call(bf16[128,1280]{1,0:T(8,128)(2,1)} %bitcast.6, f32[32,1152]{1,0:T(8,128)} %get-tuple-element.10.base_ref, f32[16,128]{1,0:T(8,128)} %get-tuple-element.11.base_max_ref, f32[16,128]{1,0:T(8,128)} %get-tuple-element.12.base_total_ref, ...), custom_call_target="tpu_custom_call" | custom-call | tf_op jit(solution)/shard_map/merge_parts/pallas_call | solution.py:417
  39.5 6.6 %all-to-all-start.1 = ((bf16[8,64,1280]{2,1,0:T(8,128)(2,1)}), bf16[8,64,1280]{2,1,0:T(8,128)(2,1)S(1)}, u32[]{:S(2)}, u32[]{:S(2)}) async-start(bf16[8,64,1280]{2,1,0:T(8,128)(2,1)} %get-tuple-element.14.own_ref), calls=%async_computation.1 | async-start | bytes 2621440 | tf_op jit(solution)/shard_map/all_to_all | solution.py:440
  47.5 16.5 %all-to-all-done.1.gathered_ref = bf16[8,64,1280]{2,1,0:T(8,128)(2,1)S(1)} async-done(((bf16[8,64,1280]{2,1,0:T(8,128)(2,1)}), bf16[8,64,1280]{2,1,0:T(8,128)(2,1)S(1)}, u32[]{:S(2)}, u32[]{:S(2)}) %all-to-all-start.1) | async-done | bytes 1310752 | tf_op jit(solution)/shard_map/all_to_all | solution.py:440
  64.0 0.0 copy-start
  64.0 1.1 %copy-done = bf16[8,64,1280]{2,1,0:T(8,128)(2,1)} copy-done((bf16[8,64,1280]{2,1,0:T(8,128)(2,1)}, bf16[8,64,1280]{2,1,0:T(8,128)(2,1)S(1)}, u32[]{:S(2)}) %copy-start) | copy-done | bytes 1310744
  65.1 3.6 %loss_grads.1 = (f32[32,1152]{1,0:T(8,128)}, f32[32,1152]{1,0:T(8,128)}) custom-call(f32[1]{0:T(128)S(6)} %copy.17.scale_ref, f32[1]{0:T(128)S(6)} %copy.18.bias_ref, bf16[8,64,1280]{2,1,0:T(8,128)(2,1)} %copy-done, bf16[8,64,1280]{2,1,0:T(8,128)(2,1)} %get-tuple-element.14.own_ref), custom_call_target="tpu_custom_call" | custom-call | tf_op jit(solution)/shard_map/loss_grads/pallas_call | solution.py:441
Async XLA Ops:
  17.6 15.2 %all-to-all-start = ((bf16[16,8,1280]{2,1,0:T(8,128)(2,1)}), bf16[16,8,1280]{2,1,0:T(8,128)(2,1)S(1)}, u32[]{:S(2)}, u32[]{:S(2)}) async-start(bf16[16,8,1280]{2,1,0:T(8,128)(2,1)} %bitcast.5), calls=%async_computation | async-start | bytes 655360 | tf_op jit(solution)/shard_map/all_to_all | solution.py:401
  32.8 0.7 %copy-start.1 = (bf16[16,8,1280]{2,1,0:T(8,128)(2,1)}, bf16[16,8,1280]{2,1,0:T(8,128)(2,1)S(1)}, u32[]{:S(2)}) copy-start(bf16[16,8,1280]{2,1,0:T(8,128)(2,1)S(1)} %all-to-all-done) | copy-start | bytes 983044
  39.5 24.5 %all-to-all-start.1 = ((bf16[8,64,1280]{2,1,0:T(8,128)(2,1)}), bf16[8,64,1280]{2,1,0:T(8,128)(2,1)S(1)}, u32[]{:S(2)}, u32[]{:S(2)}) async-start(bf16[8,64,1280]{2,1,0:T(8,128)(2,1)} %get-tuple-element.14.own_ref), calls=%async_computation.1 | async-start | bytes 2621440 | tf_op jit(solution)/shard_map/all_to_all | solution.py:440
  64.0 1.1 %copy-start = (bf16[8,64,1280]{2,1,0:T(8,128)(2,1)}, bf16[8,64,1280]{2,1,0:T(8,128)(2,1)S(1)}, u32[]{:S(2)}) copy-start(bf16[8,64,1280]{2,1,0:T(8,128)(2,1)S(1)} %all-to-all-done.1.gathered_ref) | copy-start | bytes 3932164
